TPU v7x, 32 devices: a whole 2x2x4 slice. The times are simulated.
32 devices in a mesh: groups: 2 (over y), seq: 8 (over z, x), head: 2 (over core).
Axes of the slice: x: 2, y: 2, z: 4, core: 2. Of those that a mesh axis runs over, the one named last changes fastest.
Arguments:
- queries: bfloat16 [4096, 4096], P(('groups', 'seq'), 'head'), parts along dimension 0, may hold values from -40 to 40
- key_vectors: bfloat16 [4096, 4096], P(('groups', 'seq'), 'head'), parts along dimension 0, may hold values from -6 to 6
- value_vectors: bfloat16 [4096, 4096], P(('groups', 'seq'), 'head'), parts along dimension 0, may hold values from -40 to 40
- output_grad: bfloat16 [4096, 4096], P(('groups', 'seq'), 'head'), parts along dimension 0, may hold values from -6 to 6
- norm_gain: float32 [4096], P('head'), may hold values from 0.5 to 2
- block_docs: int32 [16], P(('groups', 'seq')), parts along dimension 0, may hold values from 0 to 3, never falling along the last dimension, each value on 1 to 4 neighbouring positions
Outputs:
- normed: bfloat16 [4096, 4096], P(('groups', 'seq'), 'head'), parts along dimension 0
- query_grad: bfloat16 [4096, 4096], P(('groups', 'seq'), 'head'), parts along dimension 0
- key_grad: bfloat16 [4096, 4096], P(('groups', 'seq'), 'head'), parts along dimension 0
- value_grad: bfloat16 [4096, 4096], P(('groups', 'seq'), 'head'), parts along dimension 0
There are 2 independent parts, one for each index of `groups`. A program takes and returns all parts, laid end to end along the dimension named above; an argument that names none is the same for every part. Nothing has to cross between parts.
Inputs may be any that keep to these rules, and one draw needn't show every extreme that they name: `block_docs`: block document ids never fall along the sequence; every one of the 4 documents covers 1 to 4 blocks, and one covers exactly 4.
All inputs are finite; a program needn't handle non-finite values.
Results may differ from a plain program's by a relative error of at most 0.0058.
Values sent between devices are 32-bit elements; how exact they have to be, the bound alone decides.
No kernel may reach another device: no remote copies, remote signals or barrier semaphores. Data moves between devices by JAX's collectives and lax.ppermute only.
A program may use at most 64 MiB of HBM per device.

v0:
```python
import jax
import jax.numpy as jnp
from jax import lax
from jax.sharding import PartitionSpec as P

HEAD_DIM = 128
norm_eps = 1e-06


def spread_prefix(element, weights):
    seq_count = lax.axis_size("seq")
    flat_state = element.reshape(seq_count, -1, element.shape[-1])
    mixed = jnp.einsum(
        "ds,skc->dkc",
        weights,
        lax.all_to_all(flat_state, "seq", split_axis=0, concat_axis=0, tiled=True),
        precision=lax.Precision.HIGHEST,
    )
    returned = lax.all_to_all(mixed, "seq", split_axis=0, concat_axis=0, tiled=True)
    return returned.reshape(element.shape)


def body(queries, key_vectors, value_vectors, output_grad, norm_gain, block_docs):
    tokens, local_width = queries.shape
    heads_here = local_width // HEAD_DIM
    nblocks = block_docs.shape[0]
    block_len = tokens // nblocks
    shape_four = (nblocks, block_len, heads_here, HEAD_DIM)
    query_blk = queries.reshape(shape_four)
    key_blk = key_vectors.reshape(shape_four)
    value_blk = value_vectors.reshape(shape_four)
    tok_pos = lax.iota(jnp.int32, block_len)
    causal = (tok_pos[:, None] >= tok_pos[None, :])[None, None]
    scores = jnp.einsum("bthd,bshd->bhts", query_blk, key_blk, preferred_element_type=jnp.float32)
    att_weights = jnp.where(causal, scores, 0.0).astype(jnp.bfloat16)
    intra_out = jnp.einsum(
        "bhts,bshe->bthe", att_weights, value_blk, preferred_element_type=jnp.float32
    )
    block_kv = jnp.einsum("bshd,bshe->bhde", key_blk, value_blk, preferred_element_type=jnp.float32)
    position = lax.iota(jnp.int32, nblocks)
    same_doc = block_docs[:, None] == block_docs[None, :]
    earlier_mask = (same_doc & (position[None, :] < position[:, None])).astype(jnp.float32)
    later_mask = (same_doc & (position[None, :] > position[:, None])).astype(jnp.float32)
    local_in = jnp.einsum("kj,jhde->khde", earlier_mask, block_kv, precision=lax.Precision.HIGHEST)
    tail_weight = (block_docs == block_docs[-1]).astype(jnp.float32)
    tail_state = jnp.einsum("j,jhde->hde", tail_weight, block_kv, precision=lax.Precision.HIGHEST)
    seq_count = lax.axis_size("seq")
    all_docs = lax.all_gather(block_docs, "seq", axis=0, tiled=True).reshape(seq_count, nblocks)
    first_all = all_docs[:, 0]
    last_all = all_docs[:, -1]
    source_pos = lax.iota(jnp.int32, seq_count)
    forward_weights = (
        (source_pos[None, :] < source_pos[:, None]) & (last_all[None, :] == first_all[:, None])
    ).astype(jnp.float32)
    backward_weights = (
        (source_pos[None, :] > source_pos[:, None]) & (first_all[None, :] == last_all[:, None])
    ).astype(jnp.float32)
    carry_state = spread_prefix(tail_state, forward_weights)
    carry_use = block_docs == block_docs[0]
    states_in = (
        local_in + jnp.where(carry_use[:, None, None, None], carry_state[None], 0.0)
    ).astype(jnp.bfloat16)
    inter_out = jnp.einsum(
        "bthd,bhde->bthe", query_blk, states_in, preferred_element_type=jnp.float32
    )
    attended = (intra_out + inter_out).reshape(tokens, local_width)
    scaled_grad = norm_gain[None, :] * output_grad.astype(jnp.float32)
    square_sum, cross_sum = lax.psum(
        (jnp.sum(attended * attended, axis=1), jnp.sum(attended * scaled_grad, axis=1)), "head"
    )
    full_width = local_width * lax.axis_size("head")
    inverse_rms = lax.rsqrt(square_sum / full_width + norm_eps)
    normed = (attended * inverse_rms[:, None] * norm_gain[None, :]).astype(jnp.bfloat16)
    attended_grad = (
        inverse_rms[:, None] * scaled_grad
        - attended * (inverse_rms**3 * cross_sum / full_width)[:, None]
    )
    grad_blk = attended_grad.astype(jnp.bfloat16).reshape(shape_four)
    score_grad = jnp.einsum(
        "bthe,bshe->bhts", grad_blk, value_blk, preferred_element_type=jnp.float32
    )
    grad_weights = jnp.where(causal, score_grad, 0.0).astype(jnp.bfloat16)
    query_part = jnp.einsum(
        "bhts,bshd->bthd", grad_weights, key_blk, preferred_element_type=jnp.float32
    )
    query_part = query_part + jnp.einsum(
        "bthe,bhde->bthd", grad_blk, states_in, preferred_element_type=jnp.float32
    )
    key_intra = jnp.einsum(
        "bhts,bthd->bshd", grad_weights, query_blk, preferred_element_type=jnp.float32
    )
    value_intra = jnp.einsum(
        "bhts,bthe->bshe", att_weights, grad_blk, preferred_element_type=jnp.float32
    )
    block_grad = jnp.einsum(
        "bthd,bthe->bhde", query_blk, grad_blk, preferred_element_type=jnp.float32
    )
    grad_local = jnp.einsum(
        "kj,jhde->khde", later_mask, block_grad, precision=lax.Precision.HIGHEST
    )
    head_weight = (block_docs == block_docs[0]).astype(jnp.float32)
    head_state = jnp.einsum("j,jhde->hde", head_weight, block_grad, precision=lax.Precision.HIGHEST)
    grad_state = spread_prefix(head_state, backward_weights)
    grad_use = block_docs == block_docs[-1]
    grads_in = (
        grad_local + jnp.where(grad_use[:, None, None, None], grad_state[None], 0.0)
    ).astype(jnp.bfloat16)
    key_part = key_intra + jnp.einsum(
        "bshe,bhde->bshd", value_blk, grads_in, preferred_element_type=jnp.float32
    )
    value_part = value_intra + jnp.einsum(
        "bshd,bhde->bshe", key_blk, grads_in, preferred_element_type=jnp.float32
    )
    flat_shape = (tokens, local_width)
    return (
        normed,
        query_part.reshape(flat_shape).astype(jnp.bfloat16),
        key_part.reshape(flat_shape).astype(jnp.bfloat16),
        value_part.reshape(flat_shape).astype(jnp.bfloat16),
    )


def solution(mesh):
    in_specs = (
        P(("groups", "seq"), "head"),
        P(("groups", "seq"), "head"),
        P(("groups", "seq"), "head"),
        P(("groups", "seq"), "head"),
        P("head"),
        P(("groups", "seq")),
    )
    out_specs = (
        P(("groups", "seq"), "head"),
        P(("groups", "seq"), "head"),
        P(("groups", "seq"), "head"),
        P(("groups", "seq"), "head"),
    )
    return jax.shard_map(body, mesh=mesh, in_specs=in_specs, out_specs=out_specs, check_vma=False)
```

profile of v0, /device:TPU:0, one launch (start us, length us, event | category | flops | bytes accessed | tf_op | source)
XLA Modules:
  0.0 156.2 jit_solution(16867197169526272815)
XLA Ops:
  0.6 1.5 copy.72
  3.0 1.4 fusion.8
  4.4 7.3 %all-to-all-start = ((f32[8,256,128]{2,1,0:T(8,128)}), f32[8,256,128]{2,1,0:T(8,128)S(1)}, u32[]{:S(2)}, u32[]{:S(2)}) async-start(f32[8,256,128]{2,1,0:T(8,128)} %bitcast.3), calls=%async_computation | async-start | bytes 2097152 | tf_op jit(solution)/shard_map/all_to_all | solution.py:16
  13.7 23.9 %all-reduce = s32[8]{0:T(128)S(1)} all-reduce(s32[8]{0:T(128)S(1)} %dynamic-update-slice), channel_id=1, replica_groups=mesh['groups'=2,'seq'=8,'head'=2] {'seq'}, use_global_device_ids=true, to_apply=%add | all-reduce | flops 8 | bytes 64
  37.6 1.2 fusion.16
  38.8 1.2 copy.44
  40.0 3.6 %all-to-all-start.1 = ((f32[8,256,128]{2,1,0:T(8,128)}), f32[8,256,128]{2,1,0:T(8,128)S(1)}, u32[]{:S(2)}, u32[]{:S(2)}) async-start(f32[8,256,128]{2,1,0:T(8,128)} %copy.44), calls=%async_computation.1 | async-start | bytes 2097152 | tf_op jit(solution)/shard_map/all_to_all | solution.py:19
  43.6 1.5 copy.68
  45.1 2.4 %select_convert_fusion.1 = bf16[16,256,256]{2,1,0:T(8,128)(2,1)S(1)} fusion(bf16[256,16,128]{0,2,1:T(8,128)(2,1)S(1)} %bitcast.111, pred[256,256]{1,0:T(8,128)(4,1)S(1)} %iota_compare_fusion, bf16[256,2048]{1,0:T(8,128)(2,1)} %param.7), kind=kOutput, calls=%fused_computation.1 | convolution fusion | flops 270532608 | bytes 4259840 | tf_op jit(solution)/shard_map/bthd,bshd->bhts/dot_general | solution.py:34
  47.5 1.3 copy-done.8
  48.8 2.2 %fusion.3 = f32[16,256,128]{1,2,0:T(8,128)} fusion(bf16[16,256,256]{2,1,0:T(8,128)(2,1)S(1)} %select_convert_fusion.1, bf16[256,2048]{1,0:T(8,128)(2,1)S(1)} %copy-done), kind=kOutput, calls=%fused_computation.14 | convolution fusion | flops 268435456 | bytes 5242880 | tf_op jit(solution)/shard_map/bhts,bshe->bthe/dot_general | solution.py:36
  50.9 18.6 %all-to-all-done.1 = f32[8,256,128]{2,1,0:T(8,128)S(1)} async-done(((f32[8,256,128]{2,1,0:T(8,128)}), f32[8,256,128]{2,1,0:T(8,128)S(1)}, u32[]{:S(2)}, u32[]{:S(2)}) %all-to-all-start.1) | async-done | bytes 1048608 | tf_op jit(solution)/shard_map/all_to_all | solution.py:19
  69.5 1.5 add_convert_fusion.1
  71.4 1.8 %fusion.2 = (f32[256]{0:T(256)S(1)}, f32[16,128,256]{2,1,0:T(8,128)}) fusion(bf16[16,128,128]{2,1,0:T(8,128)(2,1)S(1)} %add_convert_fusion.1, bf16[256,16,128]{0,2,1:T(8,128)(2,1)S(1)} %bitcast.112, f32[16,256,128]{1,2,0:T(8,128)S(1)} %copy-done.7), kind=kOutput, calls=%fused_computation.7 | convolution fusion | flops 135790336 | bytes 5768192 | tf_op jit(solution)/shard_map/bthd,bhde->bthe/dot_general | solution.py:63
  73.3 1.9 %copy.47 = f32[256,2048]{1,0:T(8,128)S(1)} copy(f32[256,2048]{0,1:T(8,128)} %bitcast.116) | data formatting | bytes 4194304 | tf_op jit(solution)/shard_map/reshape | solution.py:66
  75.2 1.6 %multiply_reduce_fusion = f32[256]{0:T(256)S(1)} fusion(f32[256,2048]{1,0:T(8,128)S(1)} %copy.47, bf16[256,2048]{1,0:T(8,128)(2,1)} %param.9, f32[2048]{0:T(1024)S(1)} %copy-done.13), kind=kLoop, calls=%fused_computation.11 | loop fusion | flops 2096896 | bytes 3154944 | tf_op jit(solution)/shard_map/reduce_sum | solution.py:69
  76.8 2.5 %all-reduce.1 = (f32[256]{0:T(256)S(1)}, f32[256]{0:T(256)S(1)}) all-reduce(f32[256]{0:T(256)S(1)} %get-tuple-element.18, f32[256]{0:T(256)S(1)} %multiply_reduce_fusion), channel_id=1, replica_groups=mesh['groups'=2,'seq'=8,'head'=2] {'head'}, use_global_device_ids=true, to_apply=%region_1.2 | all-reduce | flops 512 | bytes 4096 | tf_op jit(solution)/shard_map/psum | solution.py:68
  79.3 3.6 %subtract_convert_fusion = (bf16[256,2048]{1,0:T(8,128)(2,1)}, bf16[256,2048]{1,0:T(8,128)(2,1)}) fusion(f32[256,2048]{1,0:T(8,128)S(1)} %copy.47, bf16[256,2048]{1,0:T(8,128)(2,1)} %param.9, f32[256]{0:T(256)S(1)} %get-tuple-element.16, f32[2048]{0:T(1024)S(1)} %copy-done.13, f32[256]{0:T(256)S(1)} %get-tuple-element.17), kind=kLoop, calls=%fused_computation.10 | loop fusion | flops 4718592 | bytes 5253120 | tf_op jit(solution)/shard_map/convert_element_type | solution.py:78
  82.8 1.6 %copy.69 = bf16[256,2048]{0,1:T(8,128)(2,1)S(1)} copy(bf16[256,2048]{1,0:T(8,128)(2,1)} %get-tuple-element.14) | data formatting | bytes 2097152 | tf_op jit(solution)/shard_map/reshape.36
  84.9 29.5 %all_to_all.20 = f32[8,256,128]{2,1,0:T(8,128)S(1)} all-to-all(f32[8,256,128]{2,1,0:T(8,128)S(1)} %bitcast.115), channel_id=1, replica_groups=mesh['groups'=2,'seq'=8,'head'=2] {'seq'}, dimensions={0} | all-to-all | bytes 2097152 | tf_op jit(solution)/shard_map/all_to_all | solution.py:16
  114.4 1.2 fusion.14
  115.6 1.2 copy.58
  116.7 4.4 %all-to-all-start.3 = ((f32[8,256,128]{2,1,0:T(8,128)}), f32[8,256,128]{2,1,0:T(8,128)}, u32[]{:S(2)}, u32[]{:S(2)}) async-start(f32[8,256,128]{2,1,0:T(8,128)} %copy.58), calls=%async_computation.3 | async-start | bytes 2097152 | tf_op jit(solution)/shard_map/all_to_all | solution.py:19
  123.8 1.4 fusion.1
  125.2 2.3 %copy.63 = bf16[256,2048]{1,0:T(8,128)(2,1)} copy(bf16[256,2048]{0,1:T(8,128)(2,1)} %bitcast.121) | data formatting | bytes 2097152
  127.5 3.4 %fusion.35 = f32[16,128,256]{2,1,0:T(8,128)} fusion(bf16[256,16,128]{0,2,1:T(8,128)(2,1)S(1)} %bitcast.110, bf16[16,256,256]{2,1,0:T(8,128)(2,1)} %copy-done.8), kind=kOutput, calls=%fused_computation.53 | convolution fusion | flops 268435456 | bytes 5242880 | tf_op jit(solution)/shard_map/bhts,bthe->bshe/dot_general | solution.py:92
  130.8 15.1 %all-to-all-done.3 = f32[8,256,128]{2,1,0:T(8,128)} async-done(((f32[8,256,128]{2,1,0:T(8,128)}), f32[8,256,128]{2,1,0:T(8,128)}, u32[]{:S(2)}, u32[]{:S(2)}) %all-to-all-start.3) | async-done | bytes 1048608 | tf_op jit(solution)/shard_map/all_to_all | solution.py:19
  145.9 1.7 %fusion.13 = bf16[16,128,128]{2,1,0:T(8,128)(2,1)S(1)} fusion(f32[16,128,128]{2,1,0:T(8,128)} %bitcast.18, f32[16,128,128]{1,2,0:T(8,128)} %copy-done.5), kind=kLoop, calls=%fused_computation.25 | loop fusion | flops 786432 | bytes 2621440 | tf_op jit(solution)/shard_map/convert_element_type | solution.py:107
  147.6 1.8 %fusion.5 = f32[16,128,256]{2,1,0:T(8,128)} fusion(bf16[16,128,128]{2,1,0:T(8,128)(2,1)S(1)} %fusion.13, bf16[256,2048]{1,0:T(8,128)(2,1)S(1)} %copy-done), kind=kOutput, calls=%fused_computation.16 | convolution fusion | flops 134217728 | bytes 3670016 | tf_op jit(solution)/shard_map/bshe,bhde->bshd/dot_general | solution.py:108
  150.7 1.4 copy.65
  152.1 2.7 %fusion = bf16[16,128,256]{2,1,0:T(8,128)(2,1)S(1)} fusion(f32[16,128,256]{2,1,0:T(8,128)} %fusion.5, bf16[256,16,128]{0,2,1:T(8,128)(2,1)S(1)} %bitcast.114, bf16[16,256,256]{2,1,0:T(8,128)(2,1)} %copy-done.6), kind=kOutput, calls=%fused_computation.3 | convolution fusion | flops 269484032 | bytes 6291456 | tf_op jit(solution)/shard_map/bhts,bthd->bshd/dot_general | solution.py:89
  154.8 1.4 copy.64
  (40 shorter events, 7.0 us)
Async XLA Ops:
  0.6 2.4 %copy-start = (bf16[256,2048]{1,0:T(8,128)(2,1)S(1)}, bf16[256,2048]{1,0:T(8,128)(2,1)}, u32[]{:S(2)}) copy-start(bf16[256,2048]{1,0:T(8,128)(2,1)} %param.8) | copy-start | bytes 3145732
  3.0 1.4 copy-start.3
  3.0 9.3 %copy-start.14 = (u32[32]{0:T(128)S(1)}, u32[32]{0:T(128)}, u32[]{:S(2)}) copy-start(u32[32]{0:T(128)} %constant.19) | copy-start | bytes 388
  4.4 33.2 %all-to-all-start = ((f32[8,256,128]{2,1,0:T(8,128)}), f32[8,256,128]{2,1,0:T(8,128)S(1)}, u32[]{:S(2)}, u32[]{:S(2)}) async-start(f32[8,256,128]{2,1,0:T(8,128)} %bitcast.3), calls=%async_computation | async-start | bytes 2097152 | tf_op jit(solution)/shard_map/all_to_all | solution.py:16
  40.0 29.5 %all-to-all-start.1 = ((f32[8,256,128]{2,1,0:T(8,128)}), f32[8,256,128]{2,1,0:T(8,128)S(1)}, u32[]{:S(2)}, u32[]{:S(2)}) async-start(f32[8,256,128]{2,1,0:T(8,128)} %copy.44), calls=%async_computation.1 | async-start | bytes 2097152 | tf_op jit(solution)/shard_map/all_to_all | solution.py:19
  45.0 26.0 %copy-start.1 = (bf16[256,2048]{0,1:T(8,128)(2,1)}, bf16[256,2048]{0,1:T(8,128)(2,1)S(1)}, u32[]{:S(2)}) copy-start(bf16[256,2048]{0,1:T(8,128)(2,1)S(1)} %copy.68) | copy-start | bytes 3145732
  47.5 1.3 copy-start.8
  69.5 1.9 %copy-start.7 = (f32[16,256,128]{1,2,0:T(8,128)S(1)}, f32[16,256,128]{1,2,0:T(8,128)}, u32[]{:S(2)}) copy-start(f32[16,256,128]{1,2,0:T(8,128)} %fusion.3) | copy-start | bytes 6291460
  71.4 1.8 %copy-start.10 = (bf16[16,128,128]{2,1,0:T(8,128)(2,1)}, bf16[16,128,128]{2,1,0:T(8,128)(2,1)S(1)}, u32[]{:S(2)}) copy-start(bf16[16,128,128]{2,1,0:T(8,128)(2,1)S(1)} %add_convert_fusion.1) | copy-start | bytes 1572868
  73.3 1.9 %copy-start.13 = (f32[2048]{0:T(1024)S(1)}, f32[2048]{0:T(1024)}, u32[]{:S(2)}) copy-start(f32[2048]{0:T(1024)} %param.10) | copy-start | bytes 24580
  82.8 1.6 %copy-start.2 = (bf16[256,2048]{0,1:T(8,128)(2,1)S(1)}, bf16[256,2048]{0,1:T(8,128)(2,1)}, u32[]{:S(2)}) copy-start(bf16[256,2048]{0,1:T(8,128)(2,1)} %copy-done.1) | copy-start | bytes 3145732
  84.9 30.7 %copy-start.5 = (f32[16,128,128]{1,2,0:T(8,128)}, f32[16,128,128]{1,2,0:T(8,128)S(1)}, u32[]{:S(2)}) copy-start(f32[16,128,128]{1,2,0:T(8,128)S(1)} %fusion.36) | copy-start | bytes 3145732
  116.7 29.2 %all-to-all-start.3 = ((f32[8,256,128]{2,1,0:T(8,128)}), f32[8,256,128]{2,1,0:T(8,128)}, u32[]{:S(2)}, u32[]{:S(2)}) async-start(f32[8,256,128]{2,1,0:T(8,128)} %copy.58), calls=%async_computation.3 | async-start | bytes 2097152 | tf_op jit(solution)/shard_map/all_to_all | solution.py:19
  121.1 1.2 copy-start.4
  122.4 1.3 copy-start.6
  122.4 1.4 copy-start.11
  147.6 1.9 %copy-start.9 = (f32[16,128,256]{2,1,0:T(8,128)S(1)}, f32[16,128,256]{2,1,0:T(8,128)}, u32[]{:S(2)}) copy-start(f32[16,128,256]{2,1,0:T(8,128)} %fusion.35) | copy-start | bytes 6291460
  147.6 2.6 %copy-start.12 = (bf16[256,2048]{1,0:T(8,128)(2,1)S(1)}, bf16[256,2048]{1,0:T(8,128)(2,1)}, u32[]{:S(2)}) copy-start(bf16[256,2048]{1,0:T(8,128)(2,1)} %param.7) | copy-start | bytes 3145732
where the time goes:
time: 157 us; the launch traced here: 156 us
  blocking collectives  55.9 us (36%)
  waiting for transfers between devices  33.7 us (21%)
  matrix products  21.8 us (14%)
  local copies, waits for them, and re-layouts  19.7 us (13%)
  starting transfers between devices  15.3 us (10%)
  other arithmetic  8.37 us (5%)
    all_to_all x2, waiting for transfers between devices, spread_prefix(): lax.all_to_all(mixed, 'seq', split_axis=0, concat_axis=0, tiled=True)  33.7 us
    all_to_all x1, blocking collectives, spread_prefix(): lax.all_to_all(flat_state, 'seq', split_axis=0, concat_axis=0, tiled=True)  29.5 us
    unnamed x1, blocking collectives  23.9 us
    unnamed x37, local copies, waits for them, and re-layouts  11.6 us
    all_to_all x2, starting transfers between devices, spread_prefix(): lax.all_to_all(mixed, 'seq', split_axis=0, concat_axis=0, tiled=True)  8.01 us
    all_to_all x1, starting transfers between devices, spread_prefix(): lax.all_to_all(flat_state, 'seq', split_axis=0, concat_axis=0, tiled=True)  7.25 us
    another operation x3, local copies, waits for them, and re-layouts  3.83 us
    convert_element_type x1, other arithmetic, body(): grad_blk = attended_grad.astype(jnp.bfloat16).reshape(shape_four)  3.57 us
  transfers between devices with their start and end apart: 3, of which 2 were waited for; matrix products, arithmetic and copies ran while one was open for 10% of the time, Pallas kernels for 0%

commit v1 on v0

--- a/solution.py
+++ b/solution.py
@@ -5,6 +5,22 @@
 
 HEAD_DIM = 128
 norm_eps = 1e-06
+
+
+def pairwise_exchange(shard, axis, split, join):
+    ways, here = (lax.axis_size(axis), lax.axis_index(axis))
+    width = shard.shape[split] // ways
+    shape = list(shard.shape)
+    shape[split] = width
+    height = shape[join]
+    shape[join] = height * ways
+    full = jnp.zeros(shape, shard.dtype)
+    for mask in range(ways):
+        part = lax.dynamic_slice_in_dim(shard, (here ^ mask) * width, width, axis=split)
+        if mask:
+            part = lax.ppermute(part, axis, [(d, d ^ mask) for d in range(ways)])
+        full = lax.dynamic_update_slice_in_dim(full, part, (here ^ mask) * height, axis=join)
+    return full
 
 
 def spread_prefix(element, weights):
@@ -16,7 +32,7 @@
         lax.all_to_all(flat_state, "seq", split_axis=0, concat_axis=0, tiled=True),
         precision=lax.Precision.HIGHEST,
     )
-    returned = lax.all_to_all(mixed, "seq", split_axis=0, concat_axis=0, tiled=True)
+    returned = pairwise_exchange(mixed, "seq", 0, 0)
     return returned.reshape(element.shape)
 
 

time: 157 us -> 163 us (1.038)
  blocking collectives: 55.9 us -> 26.4 us
  starting transfers between devices: 15.3 us -> 34.7 us
  waiting for transfers between devices: 33.7 us -> 48.7 us
  matrix products: 21.8 us -> 24 us
  other arithmetic: 8.37 us -> 6.69 us
    all_to_all x2 -> x0, waiting for transfers between devices: 33.7 us -> none  [spread_prefix(): lax.all_to_all(mixed, 'seq', split_axis=0, concat_axis=0, tiled=True)]
    all_to_all x1 -> x0, blocking collectives: 29.5 us -> none  [spread_prefix(): lax.all_to_all(flat_state, 'seq', split_axis=0, concat_axis=0, tiled=True)]
    ppermute x0 -> x14, waiting for transfers between devices: none -> 27.4 us  [pairwise_exchange(): part = lax.ppermute(part, axis, [(d, d ^ mask) for d in range(ways)])]
    all_to_all x1 -> x2, waiting for transfers between devices: 0.01 us -> 21.4 us  [spread_prefix(): lax.all_to_all(flat_state, 'seq', split_axis=0, concat_axis=0, tiled=True)]
    ppermute x0 -> x14, starting transfers between devices: none -> 21.2 us  [pairwise_exchange(): part = lax.ppermute(part, axis, [(d, d ^ mask) for d in range(ways)])]
    all_to_all x2 -> x0, starting transfers between devices: 8.01 us -> none  [spread_prefix(): lax.all_to_all(mixed, 'seq', split_axis=0, concat_axis=0, tiled=True)]
    all_to_all x1 -> x2, starting transfers between devices: 7.25 us -> 13.5 us  [spread_prefix(): lax.all_to_all(flat_state, 'seq', split_axis=0, concat_axis=0, tiled=True)]
    dot_general x2 -> x0, local copies, waits for them, and re-layouts: 2.32 us -> none  [spread_prefix(): jnp.einsum('ds,skc->dkc', weights, lax.all_to_all(flat_state, 'seq', spli...]
  transfers between devices with their start and end apart: 3 -> 16, of which waited for: 2 -> 6; matrix products, arithmetic and copies ran while one was open for 10% -> 11% of each run, Pallas kernels for 0% -> 0%
where the time goes in v1:
time: 163 us; the launch traced here: 162 us
  waiting for transfers between devices  48.7 us (30%)
  starting transfers between devices  34.7 us (21%)
  blocking collectives  26.4 us (16%)
  matrix products  24 us (15%)
  local copies, waits for them, and re-layouts  19.3 us (12%)
  other arithmetic  6.69 us (4%)
  between operations  1.77 us (1%)
    ppermute x14, waiting for transfers between devices, pairwise_exchange(): part = lax.ppermute(part, axis, [(d, d ^ mask) for d in range(ways)])  27.4 us
    unnamed x1, blocking collectives  23.9 us
    all_to_all x2, waiting for transfers between devices, spread_prefix(): lax.all_to_all(flat_state, 'seq', split_axis=0, concat_axis=0, tiled=True)  21.4 us
    ppermute x14, starting transfers between devices, pairwise_exchange(): part = lax.ppermute(part, axis, [(d, d ^ mask) for d in range(ways)])  21.2 us
    all_to_all x2, starting transfers between devices, spread_prefix(): lax.all_to_all(flat_state, 'seq', split_axis=0, concat_axis=0, tiled=True)  13.5 us
    unnamed x47, local copies, waits for them, and re-layouts  9.97 us
    another operation x5, local copies, waits for them, and re-layouts  3.96 us
    dot_general x2, matrix products, spread_prefix(): jnp.einsum('ds,skc->dkc', weights, lax.all_to_all(flat_state, 'seq', spli...  3.71 us
  transfers between devices with their start and end apart: 16, of which 6 were waited for; matrix products, arithmetic and copies ran while one was open for 11% of the time, Pallas kernels for 0%

profile of v1, /device:TPU:0, one launch (start us, length us, event | category | flops | bytes accessed | tf_op | source)
XLA Modules:
  0.0 161.6 jit_solution(2606163807864282826)
XLA Ops:
  0.6 1.5 copy.100
  4.4 7.3 %all-to-all-start = ((f32[8,256,128]{2,1,0:T(8,128)}), f32[8,256,128]{2,1,0:T(8,128)S(1)}, u32[]{:S(2)}, u32[]{:S(2)}) async-start(f32[8,256,128]{2,1,0:T(8,128)} %bitcast.3), calls=%async_computation | async-start | bytes 2097152 | tf_op jit(solution)/shard_map/all_to_all | solution.py:32
  13.7 23.9 %all-reduce = s32[8]{0:T(128)S(1)} all-reduce(s32[8]{0:T(128)S(1)} %dynamic-update-slice), channel_id=1, replica_groups=mesh['groups'=2,'seq'=8,'head'=2] {'seq'}, use_global_device_ids=true, to_apply=%add | all-reduce | flops 8 | bytes 64
  39.2 3.7 %select_convert_fusion.1 = bf16[16,256,256]{2,1,0:T(8,128)(2,1)} fusion(bf16[256,16,128]{0,2,1:T(8,128)(2,1)S(1)} %bitcast.127, pred[256,256]{1,0:T(8,128)(4,1)S(1)} %iota_compare_fusion, bf16[256,2048]{1,0:T(8,128)(2,1)} %param.7), kind=kOutput, calls=%fused_computation.1 | convolution fusion | flops 270532608 | bytes 4259840 | tf_op jit(solution)/shard_map/bthd,bshd->bhts/dot_general | solution.py:50
  44.8 1.5 collective-permute-start
  47.2 2.1 %collective-permute-start.2 = (f32[1,256,128]{2,0,1:T(1,128)S(1)}, f32[1,256,128]{2,0,1:T(1,128)S(1)}, u32[]{:S(2)}, u32[]{:S(2)}) collective-permute-start(f32[1,256,128]{2,0,1:T(1,128)S(1)} %get-tuple-element.28), channel_id=1, source_target_pairs={{0,6},{2,4},{4,2},{6,0},{8,14},{10,12},{12,10},{14,8},{1,7},{3,5},... | collective-permute-start | bytes 393224 | tf_op jit(solution)/shard_map/ppermute | solution.py:21
  49.3 3.8 %collective-permute-start.4 = (f32[1,256,128]{2,0,1:T(1,128)S(1)}, f32[1,256,128]{2,0,1:T(1,128)S(1)}, u32[]{:S(2)}, u32[]{:S(2)}) collective-permute-start(f32[1,256,128]{2,0,1:T(1,128)S(1)} %get-tuple-element.26), channel_id=1, source_target_pairs={{0,10},{2,8},{4,14},{6,12},{8,2},{10,0},{12,6},{14,4},{1,11},{3,9}... | collective-permute-start | bytes 393224 | tf_op jit(solution)/shard_map/ppermute | solution.py:21
  53.2 1.5 collective-permute-start.5
  54.7 1.5 collective-permute-done.1
  57.2 10.6 %collective-permute-done.3 = f32[1,256,128]{2,0,1:T(1,128)S(1)} collective-permute-done((f32[1,256,128]{2,0,1:T(1,128)S(1)}, f32[1,256,128]{2,0,1:T(1,128)S(1)}, u32[]{:S(2)}, u32[]{:S(2)}) %collective-permute-start.3) | collective-permute-done | bytes 131104 | tf_op jit(solution)/shard_map/ppermute | solution.py:21
  67.8 3.0 %collective-permute-done.4 = f32[1,256,128]{2,0,1:T(1,128)S(1)} collective-permute-done((f32[1,256,128]{2,0,1:T(1,128)S(1)}, f32[1,256,128]{2,0,1:T(1,128)S(1)}, u32[]{:S(2)}, u32[]{:S(2)}) %collective-permute-start.4) | collective-permute-done | bytes 131104 | tf_op jit(solution)/shard_map/ppermute | solution.py:21
  72.3 1.9 %fusion.2 = (f32[256]{0:T(256)S(1)}, f32[16,128,256]{2,1,0:T(8,128)}) fusion(bf16[16,128,128]{2,1,0:T(8,128)(2,1)S(1)} %add_convert_fusion.1, bf16[256,16,128]{0,2,1:T(8,128)(2,1)S(1)} %bitcast.128, f32[16,256,128]{1,2,0:T(8,128)S(1)} %fusion.3), kind=kOutput, calls=%fused_computation.7 | convolution fusion | flops 135790336 | bytes 5768192 | tf_op jit(solution)/shard_map/bthd,bhde->bthe/dot_general | solution.py:79
  74.1 1.9 %copy.68 = f32[256,2048]{1,0:T(8,128)S(1)} copy(f32[256,2048]{0,1:T(8,128)} %bitcast.132) | data formatting | bytes 4194304 | tf_op jit(solution)/shard_map/reshape | solution.py:82
  76.1 1.6 multiply_reduce_fusion
  77.7 2.5 %all-reduce.1 = (f32[256]{0:T(256)S(1)}, f32[256]{0:T(256)S(1)}) all-reduce(f32[256]{0:T(256)S(1)} %get-tuple-element.34, f32[256]{0:T(256)S(1)} %multiply_reduce_fusion), channel_id=1, replica_groups=mesh['groups'=2,'seq'=8,'head'=2] {'head'}, use_global_device_ids=true, to_apply=%region_1.2 | all-reduce | flops 512 | bytes 4096 | tf_op jit(solution)/shard_map/psum | solution.py:84
  80.2 3.6 %subtract_convert_fusion = (bf16[256,2048]{1,0:T(8,128)(2,1)}, bf16[256,2048]{1,0:T(8,128)(2,1)}) fusion(f32[256,2048]{1,0:T(8,128)S(1)} %copy.68, bf16[256,2048]{1,0:T(8,128)(2,1)} %param.9, f32[256]{0:T(256)S(1)} %get-tuple-element.32, f32[2048]{0:T(1024)S(1)} %copy-done.18, f32[256]{0:T(256)S(1)} %get-tuple-element.33), kind=kLoop, calls=%fused_computation.10 | loop fusion | flops 4718592 | bytes 5253120 | tf_op jit(solution)/shard_map/convert_element_type | solution.py:94
  83.7 1.6 copy.97
  86.7 6.3 %all-to-all-start.1 = ((f32[8,256,128]{2,1,0:T(8,128)}), f32[8,256,128]{2,1,0:T(8,128)}, u32[]{:S(2)}, u32[]{:S(2)}) async-start(f32[8,256,128]{2,1,0:T(8,128)} %bitcast.131), calls=%async_computation.1 | async-start | bytes 2097152 | tf_op jit(solution)/shard_map/all_to_all | solution.py:32
  94.6 1.8 %fusion.35 = f32[16,128,256]{2,1,0:T(8,128)} fusion(bf16[256,16,128]{0,2,1:T(8,128)(2,1)S(1)} %bitcast.125, bf16[16,256,256]{2,1,0:T(8,128)(2,1)S(1)} %copy-done.8), kind=kOutput, calls=%fused_computation.85 | convolution fusion | flops 268435456 | bytes 5242880 | tf_op jit(solution)/shard_map/bhts,bthe->bshe/dot_general | solution.py:108
  96.6 2.2 %fusion.34 = f32[16,256,128]{1,2,0:T(8,128)} fusion(bf16[16,256,256]{2,1,0:T(8,128)(2,1)S(1)} %select_convert_fusion, bf16[256,16,128]{0,2,1:T(8,128)(2,1)S(1)} %copy-done.4), kind=kOutput, calls=%fused_computation.84 | convolution fusion | flops 268435456 | bytes 5242880 | tf_op jit(solution)/shard_map/bhts,bshd->bthd/dot_general | solution.py:99
  98.8 21.4 %all-to-all-done.1 = f32[8,256,128]{2,1,0:T(8,128)} async-done(((f32[8,256,128]{2,1,0:T(8,128)}), f32[8,256,128]{2,1,0:T(8,128)}, u32[]{:S(2)}, u32[]{:S(2)}) %all-to-all-start.1) | async-done | bytes 1048608 | tf_op jit(solution)/shard_map/all_to_all | solution.py:32
  120.2 2.5 %fusion.14 = f32[8,256,128]{2,0,1:T(8,128)S(1)} fusion(f32[8,256,128]{2,1,0:T(8,128)} %all-to-all-done.1, s32[8]{0:T(128)S(1)} %all-reduce), kind=kOutput, calls=%fused_computation.26 | convolution fusion | flops 25166016 | bytes 2097184 | tf_op jit(solution)/shard_map/ds,skc->dkc/dot_general | solution.py:29
  122.7 1.5 constant_dynamic-slice_fusion
  126.1 2.3 %copy.91 = bf16[256,2048]{1,0:T(8,128)(2,1)} copy(bf16[256,2048]{0,1:T(8,128)(2,1)} %bitcast.137) | data formatting | bytes 2097152
  128.5 3.0 %collective-permute-start.9 = (f32[1,256,128]{2,0,1:T(1,128)S(1)}, f32[1,256,128]{2,0,1:T(1,128)S(1)}, u32[]{:S(2)}, u32[]{:S(2)}) collective-permute-start(f32[1,256,128]{2,0,1:T(1,128)S(1)} %copy-done.16), channel_id=1, source_target_pairs={{0,6},{2,4},{4,2},{6,0},{8,14},{10,12},{12,10},{14,8},{1,7},{3,5},... | collective-permute-start | bytes 393224 | tf_op jit(solution)/shard_map/ppermute | solution.py:21
  131.5 2.8 %collective-permute-start.11 = (f32[1,256,128]{2,0,1:T(1,128)S(1)}, f32[1,256,128]{2,0,1:T(1,128)S(1)}, u32[]{:S(2)}, u32[]{:S(2)}) collective-permute-start(f32[1,256,128]{2,0,1:T(1,128)S(1)} %copy-done.14), channel_id=1, source_target_pairs={{0,10},{2,8},{4,14},{6,12},{8,2},{10,0},{12,6},{14,4},{1,11},{3,9}... | collective-permute-start | bytes 393224 | tf_op jit(solution)/shard_map/ppermute | solution.py:21
  134.4 1.6 collective-permute-start.12
  136.9 3.4 %collective-permute-start.13 = (f32[1,256,128]{2,0,1:T(1,128)S(1)}, f32[1,256,128]{2,0,1:T(1,128)S(1)}, u32[]{:S(2)}, u32[]{:S(2)}) collective-permute-start(f32[1,256,128]{2,0,1:T(1,128)S(1)} %get-tuple-element.16), channel_id=1, source_target_pairs={{0,14},{2,12},{4,10},{6,8},{8,6},{10,4},{12,2},{14,0},{1,15},{3,13... | collective-permute-start | bytes 393224 | tf_op jit(solution)/shard_map/ppermute | solution.py:21
  140.4 9.3 %collective-permute-done.10 = f32[1,256,128]{2,0,1:T(1,128)S(1)} collective-permute-done((f32[1,256,128]{2,0,1:T(1,128)S(1)}, f32[1,256,128]{2,0,1:T(1,128)S(1)}, u32[]{:S(2)}, u32[]{:S(2)}) %collective-permute-start.10) | collective-permute-done | bytes 131104 | tf_op jit(solution)/shard_map/ppermute | solution.py:21
  149.7 3.0 %collective-permute-done.11 = f32[1,256,128]{2,0,1:T(1,128)S(1)} collective-permute-done((f32[1,256,128]{2,0,1:T(1,128)S(1)}, f32[1,256,128]{2,0,1:T(1,128)S(1)}, u32[]{:S(2)}, u32[]{:S(2)}) %collective-permute-start.11) | collective-permute-done | bytes 131104 | tf_op jit(solution)/shard_map/ppermute | solution.py:21
  152.9 1.8 %fusion.5 = f32[16,128,256]{2,1,0:T(8,128)} fusion(bf16[16,128,128]{2,1,0:T(8,128)(2,1)S(1)} %fusion.13, bf16[256,2048]{1,0:T(8,128)(2,1)S(1)} %copy-done), kind=kOutput, calls=%fused_computation.16 | convolution fusion | flops 134217728 | bytes 3670016 | tf_op jit(solution)/shard_map/bshe,bhde->bshd/dot_general | solution.py:124
  157.5 2.7 %fusion = bf16[16,128,256]{2,1,0:T(8,128)(2,1)S(1)} fusion(f32[16,128,256]{2,1,0:T(8,128)} %fusion.5, bf16[256,16,128]{0,2,1:T(8,128)(2,1)S(1)} %bitcast.130, bf16[16,256,256]{2,1,0:T(8,128)(2,1)} %copy-done.6), kind=kOutput, calls=%fused_computation.3 | convolution fusion | flops 269484032 | bytes 6291456 | tf_op jit(solution)/shard_map/bhts,bthd->bshd/dot_general | solution.py:105
  (93 shorter events, 20.9 us)
Async XLA Ops:
  0.6 2.4 %copy-start = (bf16[256,2048]{1,0:T(8,128)(2,1)S(1)}, bf16[256,2048]{1,0:T(8,128)(2,1)}, u32[]{:S(2)}) copy-start(bf16[256,2048]{1,0:T(8,128)(2,1)} %param.8) | copy-start | bytes 3145732
  3.0 9.3 %copy-start.19 = (u32[32]{0:T(128)S(1)}, u32[32]{0:T(128)}, u32[]{:S(2)}) copy-start(u32[32]{0:T(128)} %constant.44) | copy-start | bytes 388
  4.4 38.4 %all-to-all-start = ((f32[8,256,128]{2,1,0:T(8,128)}), f32[8,256,128]{2,1,0:T(8,128)S(1)}, u32[]{:S(2)}, u32[]{:S(2)}) async-start(f32[8,256,128]{2,1,0:T(8,128)} %bitcast.3), calls=%async_computation | async-start | bytes 2097152 | tf_op jit(solution)/shard_map/all_to_all | solution.py:32
  39.1 33.2 %copy-start.1 = (bf16[256,2048]{0,1:T(8,128)(2,1)}, bf16[256,2048]{0,1:T(8,128)(2,1)S(1)}, u32[]{:S(2)}) copy-start(bf16[256,2048]{0,1:T(8,128)(2,1)S(1)} %copy.96) | copy-start | bytes 3145732
  42.9 3.4 %copy-start.7 = (bf16[16,256,256]{2,1,0:T(8,128)(2,1)S(1)}, bf16[16,256,256]{2,1,0:T(8,128)(2,1)}, u32[]{:S(2)}) copy-start(bf16[16,256,256]{2,1,0:T(8,128)(2,1)} %select_convert_fusion.1) | copy-start | bytes 6291460
  44.8 8.4 %collective-permute-start = (f32[1,256,128]{2,0,1:T(1,128)S(1)}, f32[1,256,128]{2,0,1:T(1,128)S(1)}, u32[]{:S(2)}, u32[]{:S(2)}) collective-permute-start(f32[1,256,128]{2,0,1:T(1,128)S(1)} %get-tuple-element.30), channel_id=1, source_target_pairs={{0,2},{2,0},{4,6},{6,4},{8,10},{10,8},{12,14},{14,12},{1,3},{3,1},... | collective-permute-start | bytes 393224 | tf_op jit(solution)/shard_map/ppermute | solution.py:21
  47.1 9.1 %collective-permute-start.1 = (f32[1,256,128]{2,0,1:T(1,128)S(1)}, f32[1,256,128]{2,0,1:T(1,128)S(1)}, u32[]{:S(2)}, u32[]{:S(2)}) collective-permute-start(f32[1,256,128]{2,0,1:T(1,128)S(1)} %get-tuple-element.29), channel_id=1, source_target_pairs={{0,4},{2,6},{4,0},{6,2},{8,12},{10,14},{12,8},{14,10},{1,5},{3,7},... | collective-permute-start | bytes 393224 | tf_op jit(solution)/shard_map/ppermute | solution.py:21
  47.2 10.0 %collective-permute-start.2 = (f32[1,256,128]{2,0,1:T(1,128)S(1)}, f32[1,256,128]{2,0,1:T(1,128)S(1)}, u32[]{:S(2)}, u32[]{:S(2)}) collective-permute-start(f32[1,256,128]{2,0,1:T(1,128)S(1)} %get-tuple-element.28), channel_id=1, source_target_pairs={{0,6},{2,4},{4,2},{6,0},{8,14},{10,12},{12,10},{14,8},{1,7},{3,5},... | collective-permute-start | bytes 393224 | tf_op jit(solution)/shard_map/ppermute | solution.py:21
  49.3 18.5 %collective-permute-start.3 = (f32[1,256,128]{2,0,1:T(1,128)S(1)}, f32[1,256,128]{2,0,1:T(1,128)S(1)}, u32[]{:S(2)}, u32[]{:S(2)}) collective-permute-start(f32[1,256,128]{2,0,1:T(1,128)S(1)} %get-tuple-element.27), channel_id=1, source_target_pairs={{0,8},{2,10},{4,12},{6,14},{8,0},{10,2},{12,4},{14,6},{1,9},{3,11}... | collective-permute-start | bytes 393224 | tf_op jit(solution)/shard_map/ppermute | solution.py:21
  49.3 21.5 %collective-permute-start.4 = (f32[1,256,128]{2,0,1:T(1,128)S(1)}, f32[1,256,128]{2,0,1:T(1,128)S(1)}, u32[]{:S(2)}, u32[]{:S(2)}) collective-permute-start(f32[1,256,128]{2,0,1:T(1,128)S(1)} %get-tuple-element.26), channel_id=1, source_target_pairs={{0,10},{2,8},{4,14},{6,12},{8,2},{10,0},{12,6},{14,4},{1,11},{3,9}... | collective-permute-start | bytes 393224 | tf_op jit(solution)/shard_map/ppermute | solution.py:21
  53.2 17.7 %collective-permute-start.5 = (f32[1,256,128]{2,0,1:T(1,128)S(1)}, f32[1,256,128]{2,0,1:T(1,128)S(1)}, u32[]{:S(2)}, u32[]{:S(2)}) collective-permute-start(f32[1,256,128]{2,0,1:T(1,128)S(1)} %get-tuple-element.25), channel_id=1, source_target_pairs={{0,12},{2,14},{4,8},{6,10},{8,4},{10,6},{12,0},{14,2},{1,13},{3,15... | collective-permute-start | bytes 393224 | tf_op jit(solution)/shard_map/ppermute | solution.py:21
  56.2 14.7 %collective-permute-start.6 = (f32[1,256,128]{2,0,1:T(1,128)S(1)}, f32[1,256,128]{2,0,1:T(1,128)S(1)}, u32[]{:S(2)}, u32[]{:S(2)}) collective-permute-start(f32[1,256,128]{2,0,1:T(1,128)S(1)} %get-tuple-element.24), channel_id=1, source_target_pairs={{0,14},{2,12},{4,10},{6,8},{8,6},{10,4},{12,2},{14,0},{1,15},{3,13... | collective-permute-start | bytes 393224 | tf_op jit(solution)/shard_map/ppermute | solution.py:21
  74.1 1.9 %copy-start.18 = (f32[2048]{0:T(1024)S(1)}, f32[2048]{0:T(1024)}, u32[]{:S(2)}) copy-start(f32[2048]{0:T(1024)} %param.10) | copy-start | bytes 24580
  86.7 33.5 %all-to-all-start.1 = ((f32[8,256,128]{2,1,0:T(8,128)}), f32[8,256,128]{2,1,0:T(8,128)}, u32[]{:S(2)}, u32[]{:S(2)}) async-start(f32[8,256,128]{2,1,0:T(8,128)} %bitcast.131), calls=%async_computation.1 | async-start | bytes 2097152 | tf_op jit(solution)/shard_map/all_to_all | solution.py:32
  94.6 2.0 %copy-start.6 = (bf16[16,256,256]{2,1,0:T(8,128)(2,1)}, bf16[16,256,256]{2,1,0:T(8,128)(2,1)S(1)}, u32[]{:S(2)}) copy-start(bf16[16,256,256]{2,1,0:T(8,128)(2,1)S(1)} %select_convert_fusion) | copy-start | bytes 6291460
  94.6 2.1 %copy-start.4 = (bf16[256,16,128]{0,2,1:T(8,128)(2,1)S(1)}, bf16[256,16,128]{0,2,1:T(8,128)(2,1)}, u32[]{:S(2)}) copy-start(bf16[256,16,128]{0,2,1:T(8,128)(2,1)} %copy-done.3) | copy-start | bytes 3145732
  120.2 4.5 %copy-start.10 = (f32[16,256,128]{1,2,0:T(8,128)S(1)}, f32[16,256,128]{1,2,0:T(8,128)}, u32[]{:S(2)}) copy-start(f32[16,256,128]{1,2,0:T(8,128)} %fusion.34) | copy-start | bytes 6291460
  120.2 4.5 %copy-start.12 = (bf16[16,128,128]{2,1,0:T(8,128)(2,1)S(1)}, bf16[16,128,128]{2,1,0:T(8,128)(2,1)}, u32[]{:S(2)}) copy-start(bf16[16,128,128]{2,1,0:T(8,128)(2,1)} %copy-done.11) | copy-start | bytes 1572868
  124.3 10.1 %collective-permute-start.7 = (f32[1,256,128]{2,0,1:T(1,128)}, f32[1,256,128]{2,0,1:T(1,128)}, u32[]{:S(2)}, u32[]{:S(2)}) collective-permute-start(f32[1,256,128]{2,0,1:T(1,128)} %get-tuple-element.22), channel_id=1, source_target_pairs={{0,2},{2,0},{4,6},{6,4},{8,10},{10,8},{12,14},{14,12},{1,3},{3,1},... | collective-permute-start | bytes 393224 | tf_op jit(solution)/shard_map/ppermute | solution.py:21
  126.1 2.3 %copy-start.17 = (f32[1,256,128]{2,0,1:T(1,128)S(1)}, f32[1,256,128]{2,0,1:T(1,128)}, u32[]{:S(2)}) copy-start(f32[1,256,128]{2,0,1:T(1,128)} %get-tuple-element.21) | copy-start | bytes 393220
  126.1 2.4 %copy-start.16 = (f32[1,256,128]{2,0,1:T(1,128)S(1)}, f32[1,256,128]{2,0,1:T(1,128)}, u32[]{:S(2)}) copy-start(f32[1,256,128]{2,0,1:T(1,128)} %get-tuple-element.20) | copy-start | bytes 393220
  126.1 5.4 %copy-start.15 = (f32[1,256,128]{2,0,1:T(1,128)S(1)}, f32[1,256,128]{2,0,1:T(1,128)}, u32[]{:S(2)}) copy-start(f32[1,256,128]{2,0,1:T(1,128)} %get-tuple-element.19) | copy-start | bytes 393220
  126.1 5.4 %copy-start.14 = (f32[1,256,128]{2,0,1:T(1,128)S(1)}, f32[1,256,128]{2,0,1:T(1,128)}, u32[]{:S(2)}) copy-start(f32[1,256,128]{2,0,1:T(1,128)} %get-tuple-element.18) | copy-start | bytes 393220
  128.4 24.3 %copy-start.5 = (f32[16,128,128]{1,2,0:T(8,128)S(1)}, f32[16,128,128]{1,2,0:T(8,128)}, u32[]{:S(2)}) copy-start(f32[16,128,128]{1,2,0:T(8,128)} %fusion.36) | copy-start | bytes 3145732
  128.4 8.5 %collective-permute-start.8 = (f32[1,256,128]{2,0,1:T(1,128)S(1)}, f32[1,256,128]{2,0,1:T(1,128)S(1)}, u32[]{:S(2)}, u32[]{:S(2)}) collective-permute-start(f32[1,256,128]{2,0,1:T(1,128)S(1)} %copy-done.17), channel_id=1, source_target_pairs={{0,4},{2,6},{4,0},{6,2},{8,12},{10,14},{12,8},{14,10},{1,5},{3,7},... | collective-permute-start | bytes 393224 | tf_op jit(solution)/shard_map/ppermute | solution.py:21
  128.5 11.9 %collective-permute-start.9 = (f32[1,256,128]{2,0,1:T(1,128)S(1)}, f32[1,256,128]{2,0,1:T(1,128)S(1)}, u32[]{:S(2)}, u32[]{:S(2)}) collective-permute-start(f32[1,256,128]{2,0,1:T(1,128)S(1)} %copy-done.16), channel_id=1, source_target_pairs={{0,6},{2,4},{4,2},{6,0},{8,14},{10,12},{12,10},{14,8},{1,7},{3,5},... | collective-permute-start | bytes 393224 | tf_op jit(solution)/shard_map/ppermute | solution.py:21
  131.5 18.2 %collective-permute-start.10 = (f32[1,256,128]{2,0,1:T(1,128)S(1)}, f32[1,256,128]{2,0,1:T(1,128)S(1)}, u32[]{:S(2)}, u32[]{:S(2)}) collective-permute-start(f32[1,256,128]{2,0,1:T(1,128)S(1)} %copy-done.15), channel_id=1, source_target_pairs={{0,8},{2,10},{4,12},{6,14},{8,0},{10,2},{12,4},{14,6},{1,9},{3,11}... | collective-permute-start | bytes 393224 | tf_op jit(solution)/shard_map/ppermute | solution.py:21
  131.5 21.2 %collective-permute-start.11 = (f32[1,256,128]{2,0,1:T(1,128)S(1)}, f32[1,256,128]{2,0,1:T(1,128)S(1)}, u32[]{:S(2)}, u32[]{:S(2)}) collective-permute-start(f32[1,256,128]{2,0,1:T(1,128)S(1)} %copy-done.14), channel_id=1, source_target_pairs={{0,10},{2,8},{4,14},{6,12},{8,2},{10,0},{12,6},{14,4},{1,11},{3,9}... | collective-permute-start | bytes 393224 | tf_op jit(solution)/shard_map/ppermute | solution.py:21
  134.4 18.3 %collective-permute-start.12 = (f32[1,256,128]{2,0,1:T(1,128)S(1)}, f32[1,256,128]{2,0,1:T(1,128)S(1)}, u32[]{:S(2)}, u32[]{:S(2)}) collective-permute-start(f32[1,256,128]{2,0,1:T(1,128)S(1)} %get-tuple-element.17), channel_id=1, source_target_pairs={{0,12},{2,14},{4,8},{6,10},{8,4},{10,6},{12,0},{14,2},{1,13},{3,15... | collective-permute-start | bytes 393224 | tf_op jit(solution)/shard_map/ppermute | solution.py:21
  136.9 15.8 %collective-permute-start.13 = (f32[1,256,128]{2,0,1:T(1,128)S(1)}, f32[1,256,128]{2,0,1:T(1,128)S(1)}, u32[]{:S(2)}, u32[]{:S(2)}) collective-permute-start(f32[1,256,128]{2,0,1:T(1,128)S(1)} %get-tuple-element.16), channel_id=1, source_target_pairs={{0,14},{2,12},{4,10},{6,8},{8,6},{10,4},{12,2},{14,0},{1,15},{3,13... | collective-permute-start | bytes 393224 | tf_op jit(solution)/shard_map/ppermute | solution.py:21
  152.9 1.9 %copy-start.9 = (f32[16,128,256]{2,1,0:T(8,128)S(1)}, f32[16,128,256]{2,1,0:T(8,128)}, u32[]{:S(2)}) copy-start(f32[16,128,256]{2,1,0:T(8,128)} %fusion.35) | copy-start | bytes 6291460
  152.9 2.6 %copy-start.13 = (bf16[256,2048]{1,0:T(8,128)(2,1)S(1)}, bf16[256,2048]{1,0:T(8,128)(2,1)}, u32[]{:S(2)}) copy-start(bf16[256,2048]{1,0:T(8,128)(2,1)} %param.7) | copy-start | bytes 3145732
  (4 other events, 6.5 us)
